TPU v7x, 512 devices: a whole 4x4x16 slice. The times are simulated.
512 devices in a mesh: frame: 8 (over y, core), row: 8 (over z_lo), col: 8 (over x, z_hi).
Axes of the slice: x: 4, y: 4, z: 16 (z_hi: 2, z_lo: 8; z = z_hi * 8 + z_lo), core: 2. Of those that a mesh axis runs over, the one named last changes fastest.
Arguments:
- frames_in: bfloat16 [32, 64, 64, 1024], P('frame', 'row', None, 'col'), may hold values from -6 to 6
- spatial_weight: bfloat16 [9, 1024, 1024], P(None, ('frame', 'row'), 'col'), may hold values from -0.0625 to 0.0625
- temporal_weight: bfloat16 [3, 1024, 1024], P(None, ('frame', 'row'), 'col'), may hold values from -0.109375 to 0.109375
- spatial_bias: float32 [1024], P('col'), may hold values from -3 to 3
- temporal_bias: float32 [1024], P('col'), may hold values from -3 to 3
- clip_id: int32 [32], replicated, may hold values from 0 to 7, as said below
Outputs:
- block_out: bfloat16 [32, 64, 64, 1024], P('frame', 'row', None, 'col')
Inputs may be any that keep to these rules, and one draw needn't show every extreme that they name: `clip_id`: clip numbers of the frames in order, never falling; each clip has 1 to 7 frames and one has exactly 7.
All inputs are finite; a program needn't handle non-finite values.
Results may differ from a plain program's by a relative error of at most 0.01.
Values may be sent and summed in bfloat16 or wider, within the bound.
A program may use at most 64 MiB of HBM per device.

v0:
```python
import jax
import jax.numpy as jnp
from jax import lax
from jax.sharding import PartitionSpec as P


def with_halo(block, sides, width):
    for axis, dim in sides:
        count = lax.axis_size(axis)
        forward = [(i, i + 1) for i in range(count - 1)]
        backward = [(target, source) for source, target in forward]
        low = lax.ppermute(
            lax.slice_in_dim(block, block.shape[dim] - width, None, axis=dim), axis, forward
        )
        high = lax.ppermute(lax.slice_in_dim(block, 0, width, axis=dim), axis, backward)
        block = jnp.concatenate([low, block, high], axis=dim)
    return block


def spatial_terms(total, gathered, weights):
    row_count = total.shape[1]
    wide = total.shape[2]
    for tap in range(9):
        shift_y, shift_x = (tap // 3, tap % 3)
        window = gathered[:, shift_y : shift_y + row_count, shift_x : shift_x + wide, :]
        total = total + jnp.einsum(
            "fhwc,cd->fhwd", window, weights[tap], preferred_element_type=jnp.float32
        )
    return total


def temporal_terms(sources, weights):
    result = []
    for tap in range(3):
        window = sources[tap]
        result.append(
            jnp.einsum("fhwc,cd->fhwd", window, weights[tap], preferred_element_type=jnp.float32)
        )
    return (result[0], result[1], result[2])


def body(frames_in, spatial_weight, temporal_weight, spatial_bias, temporal_bias, clip_id):
    fr_count, row_count, wide, col_width = frames_in.shape
    rimmed = with_halo(frames_in, (("row", 1),), 1)
    gathered = lax.all_gather(rimmed, "col", axis=3, tiled=True)
    gathered = jnp.pad(gathered, ((0, 0), (0, 0), (1, 1), (0, 0)))
    blank = jnp.zeros((fr_count, row_count, wide, col_width), jnp.float32)
    full_spatial, full_temporal = (
        lax.all_gather(spatial_weight, ("frame", "row"), axis=1, tiled=True),
        lax.all_gather(temporal_weight, ("frame", "row"), axis=1, tiled=True),
    )
    spatial = spatial_terms(blank, gathered, full_spatial)
    hidden = (spatial + spatial_bias).astype(jnp.bfloat16)
    active = jax.nn.silu(hidden.astype(jnp.float32)).astype(jnp.bfloat16)
    index = lax.axis_index("frame")
    edge_ids = jnp.full((1,), -1, jnp.int32)
    padded_ids = jnp.concatenate([edge_ids, clip_id, edge_ids])
    local_ids = lax.dynamic_slice_in_dim(padded_ids, index * fr_count, fr_count + 2)
    prev_ok = (local_ids[1:-1] == local_ids[:-2]).astype(jnp.float32).reshape(fr_count, 1, 1, 1)
    next_ok = (local_ids[1:-1] == local_ids[2:]).astype(jnp.float32).reshape(fr_count, 1, 1, 1)
    source = with_halo(active, (("frame", 0),), 1)
    whole = lax.all_gather(source, "col", axis=3, tiled=True)
    sources = (whole[:-2], whole[1:-1], whole[2:])
    taps = temporal_terms(sources, full_temporal)
    before, after = (taps[0], taps[2])
    total = (
        hidden.astype(jnp.float32) + temporal_bias + prev_ok * before + taps[1] + next_ok * after
    )
    return total.astype(jnp.bfloat16)


def solution(mesh):
    placed = (
        P("frame", "row", None, "col"),
        P(None, ("frame", "row"), "col"),
        P(None, ("frame", "row"), "col"),
        P("col"),
        P("col"),
        P(),
    )
    return jax.shard_map(
        body, mesh=mesh, in_specs=placed, out_specs=P("frame", "row", None, "col"), check_vma=False
    )
```

profile of v0, /device:TPU:266, one launch (start us, length us, event | category | flops | bytes accessed | tf_op | source)
XLA Modules:
  0.0 734.2 jit_solution(9733512047469235792)
XLA Ops:
  6.5 0.0 all-gather.6.cloned.1.call-start
  6.5 0.7 all-gather.6.cloned.1.call-update
  7.3 0.0 all-gather.4.cloned.1.call-start
  7.3 0.9 fusion.65
  8.2 2.9 collective-permute-start
  11.1 1.3 collective-permute-start.1
  12.4 0.6 collective-permute-done
  13.0 4.3 collective-permute-done.1
  17.3 2.0 pad_maximum_fusion.1
  19.3 0.0 all-gather.4.cloned.1.call-update
  19.3 0.0 all-gather.8.cloned.1.call-start
  19.4 142.3 %all-gather.6.cloned.1.call-done = bf16[9,1024,128]{2,1,0:T(8,128)(2,1)} async-done(((bf16[9,16,128]{2,1,0:T(8,128)(2,1)}), bf16[9,1024,128]{2,1,0:T(8,128)(2,1)}) %all-gather.6.cloned.1.call-update) | async-done | bytes 2359312 | tf_op jit(solution)/shard_map/all_gather | solution.py:49
  161.7 175.7 %all-gather.4.cloned.1.call-done = bf16[4,10,64,1024]{3,2,1,0:T(8,128)(2,1)} async-done(((bf16[4,10,64,128]{3,2,1,0:T(8,128)(2,1)}), bf16[4,10,64,1024]{3,2,1,0:T(8,128)(2,1)}) %all-gather.4.cloned.1.call-update) | async-done | bytes 5242896 | tf_op jit(solution)/shard_map/all_gather | solution.py:45
  337.4 0.0 copy-start
  337.4 0.0 copy-start.2
  337.4 3.6 fusion
  341.1 0.2 copy-done
  341.3 2.2 fusion.2
  343.5 0.0 copy-done.2
  343.5 1.3 fusion.4
  344.8 1.3 fusion.55
  346.1 1.3 fusion.56
  347.3 1.3 fusion.57
  348.6 0.0 copy-start.5
  348.6 1.3 fusion.6
  349.9 1.3 fusion.8
  351.1 0.0 copy-done.5
  351.1 0.0 copy-start.6
  351.2 0.0 copy-start.3
  351.2 1.9 fusion.54
  353.1 0.0 copy-start.4
  353.2 1.9 collective-permute-start.2
  355.1 3.6 collective-permute-start.3
  358.7 0.7 collective-permute-done.2
  359.5 1.8 collective-permute-done.3
  361.2 1.0 pad_maximum_fusion
  362.2 0.0 all-gather.8.cloned.1.call-update
  362.3 0.0 copy-done.6
  362.3 0.1 pad_add_fusion
  362.3 0.1 dynamic_slice.3
  362.4 0.1 compare_convert_fusion.1
  362.5 0.0 copy-done.3
  362.5 355.9 %all_gather.15 = bf16[3,1024,128]{2,1,0:T(8,128)(2,1)S(1)} all-gather(bf16[3,16,128]{2,1,0:T(8,128)(2,1)S(1)} %copy-done.3), channel_id=1, replica_groups=mesh['frame'=8,'row'=8,'col'=8] {'frame','row'}, dimensions={1}, use_global_device_ids=true | all-gather | bytes 798720 | tf_op jit(solution)/shard_map/all_gather | solution.py:50
  718.4 3.6 convolution_multiply_fusion
  722.0 0.0 copy-done.4
  722.0 3.4 fusion.19
  725.5 0.0 copy-done.1
  725.5 2.1 fusion.50
  (3 shorter events, 0.0 us)
Async XLA Ops:
  6.5 155.2 %all-gather.6.cloned.1.call-start = ((), (), s32[]{:S(2)}) async-start(), calls=%async_computation.1 | async-start | bytes 2396160 | tf_op jit(solution)/shard_map/all_gather | solution.py:49
  7.3 330.2 %all-gather.4.cloned.1.call-start = ((), (), s32[]{:S(2)}) async-start(), calls=%async_computation | async-start | bytes 5898240 | tf_op jit(solution)/shard_map/all_gather | solution.py:45
  8.2 4.8 collective-permute-start
  11.1 6.2 collective-permute-start.1
  19.3 699.1 %all-gather.8.cloned.1.call-start = ((), (), s32[]{:S(2)}) async-start(), calls=%async_computation.2 | async-start | bytes 7077888 | tf_op jit(solution)/shard_map/all_gather | solution.py:62
  337.4 3.8 copy-start
  337.4 6.1 copy-start.2
  348.6 2.6 copy-start.5
  351.1 11.1 %copy-start.6 = (s32[32]{0:T(128)S(1)}, s32[32]{0:T(128)}, u32[]{:S(2)}) copy-start(s32[32]{0:T(128)} %param.11) | copy-start | bytes 388
  351.2 11.3 %copy-start.3 = (bf16[3,16,128]{2,1,0:T(8,128)(2,1)S(1)}, bf16[3,16,128]{2,1,0:T(8,128)(2,1)}, u32[]{:S(2)}) copy-start(bf16[3,16,128]{2,1,0:T(8,128)(2,1)} %param.8) | copy-start | bytes 36868
  353.1 368.9 %copy-start.4 = (f32[128]{0:T(128)S(1)}, f32[128]{0:T(128)}, u32[]{:S(2)}) copy-start(f32[128]{0:T(128)} %param.10) | copy-start | bytes 1540
  353.2 6.3 collective-permute-start.2
  355.1 6.1 collective-permute-start.3
  718.4 7.1 copy-start.1
Sparse Core Ops, SparseCore 0:
  9.4 152.2 all-gather.5
  164.8 172.6 all-gather.3
  362.4 233.3 all-gather.7
where the time goes:
time: 734 us
  blocking collectives  356 us (49%)
  waiting for transfers between devices  326 us (44%)
  matrix products  24.6 us (3%)
  between operations  13.3 us (2%)
  starting transfers between devices  9.86 us (1%)
    all_gather x1, blocking collectives, body(): lax.all_gather(temporal_weight, ('frame', 'row'), axis=1, tiled=True)  356 us
    all_gather x1, waiting for transfers between devices, body(): gathered = lax.all_gather(rimmed, 'col', axis=3, tiled=True)  176 us
    all_gather x1, waiting for transfers between devices, body(): lax.all_gather(spatial_weight, ('frame', 'row'), axis=1, tiled=True)  142 us
    dot_general x9, matrix products, spatial_terms(): jnp.einsum('fhwc,cd->fhwd', window, weights[tap], preferred_element_type=...  15.4 us
  transfers between devices with their start and end apart: 7, of which 6 were waited for; matrix products, arithmetic and copies ran while one was open for 0% of the time, Pallas kernels for 0%

commit v1 on v0

--- a/solution.py
+++ b/solution.py
@@ -42,7 +42,9 @@
 def body(frames_in, spatial_weight, temporal_weight, spatial_bias, temporal_bias, clip_id):
     fr_count, row_count, wide, col_width = frames_in.shape
     rimmed = with_halo(frames_in, (("row", 1),), 1)
-    gathered = lax.all_gather(rimmed, "col", axis=3, tiled=True)
+    z2 = jnp.stack(lax.psum(1, "col") * [rimmed])
+    w2 = lax.all_to_all(z2, "col", 0, 0)
+    gathered = jnp.concatenate(w2, axis=3)
     gathered = jnp.pad(gathered, ((0, 0), (0, 0), (1, 1), (0, 0)))
     blank = jnp.zeros((fr_count, row_count, wide, col_width), jnp.float32)
     full_spatial, full_temporal = (

time: 734 us -> 754 us (1.027)
  the two profiles are of different devices: /device:TPU:266 before, /device:TPU:4 now
where the time goes in v1:
time: 754 us; the launch traced here: 753 us
  waiting for transfers between devices  354 us (47%)
  blocking collectives  315 us (42%)
  matrix products  30.6 us (4%)
  starting transfers between devices  26 us (3%)
  between operations  13.6 us (2%)
  local copies, waits for them, and re-layouts  10.7 us (1%)
    all_gather x1, blocking collectives, body(): lax.all_gather(temporal_weight, ('frame', 'row'), axis=1, tiled=True)  315 us
    all_gather x1, waiting for transfers between devices, body(): lax.all_gather(spatial_weight, ('frame', 'row'), axis=1, tiled=True)  236 us
    all_to_all x1, waiting for transfers between devices, body(): w2 = lax.all_to_all(z2, 'col', 0, 0)  109 us
    dot_general x9, matrix products, spatial_terms(): jnp.einsum('fhwc,cd->fhwd', window, weights[tap], preferred_element_type=...  21.4 us
    all_to_all x1, starting transfers between devices, body(): w2 = lax.all_to_all(z2, 'col', 0, 0)  17.2 us
  transfers between devices with their start and end apart: 7, of which 5 were waited for; matrix products, arithmetic and copies ran while one was open for 1% of the time, Pallas kernels for 0%

profile of v1, /device:TPU:4, one launch (start us, length us, event | category | flops | bytes accessed | tf_op | source)
XLA Modules:
  0.0 753.1 jit_solution(620829263147515091)
XLA Ops:
  6.5 0.9 fusion.39
  7.4 3.8 collective-permute-start
  11.3 1.3 collective-permute-start.1
  12.6 0.6 collective-permute-done
  13.1 4.3 collective-permute-done.1
  17.4 1.1 pad_maximum_fusion.1
  18.5 3.7 stack.2
  22.2 17.2 %all-to-all-start = ((bf16[8,4,10,64,128]{4,3,2,1,0:T(8,128)(2,1)}), bf16[8,4,10,64,128]{4,3,2,1,0:T(8,128)(2,1)}, u32[]{:S(2)}, u32[]{:S(2)}) async-start(bf16[8,4,10,64,128]{4,3,2,1,0:T(8,128)(2,1)} %stack.2), calls=%async_computation | async-start | bytes 10485760 | tf_op jit(solution)/shard_map/all_to_all | solution.py:46
  39.4 0.0 all-gather.3.cloned.1.call-start
  39.4 0.7 all-gather.3.cloned.1.call-update
  40.1 0.0 all-gather.5.cloned.1.call-start
  40.2 109.4 %all-to-all-done = bf16[8,4,10,64,128]{4,3,2,1,0:T(8,128)(2,1)} async-done(((bf16[8,4,10,64,128]{4,3,2,1,0:T(8,128)(2,1)}), bf16[8,4,10,64,128]{4,3,2,1,0:T(8,128)(2,1)}, u32[]{:S(2)}, u32[]{:S(2)}) %all-to-all-start) | async-done | bytes 5242912 | tf_op jit(solution)/shard_map/all_to_all | solution.py:46
  149.6 5.8 copy_bitcast_fusion
  155.4 235.9 %all-gather.3.cloned.1.call-done = bf16[9,1024,128]{2,1,0:T(8,128)(2,1)} async-done(((bf16[9,16,128]{2,1,0:T(8,128)(2,1)}), bf16[9,1024,128]{2,1,0:T(8,128)(2,1)}) %all-gather.3.cloned.1.call-update) | async-done | bytes 2359312 | tf_op jit(solution)/shard_map/all_gather | solution.py:51
  391.3 0.0 copy-start.1
  391.3 3.6 fusion.10
  395.0 0.2 copy-done.1
  395.1 2.2 fusion.6
  397.4 0.0 copy-done.2
  397.4 1.3 fusion.8
  398.7 1.3 fusion.2
  399.9 1.3 fusion.4
  401.2 1.3 fusion
  402.5 3.5 fusion.25
  406.0 0.0 copy-start.5
  406.0 3.5 fusion.23
  409.5 0.0 copy-done.5
  409.5 0.0 copy-start.6
  409.5 0.0 copy-start.3
  409.6 3.5 fusion.31
  413.1 0.0 copy-start.4
  413.1 2.2 collective-permute-start.2
  415.3 1.5 collective-permute-start.3
  416.8 0.0 collective-permute-done.2
  416.8 3.5 collective-permute-done.3
  420.3 1.0 pad_maximum_fusion
  421.3 0.0 all-gather.5.cloned.1.call-update
  421.4 0.0 copy-done.6
  421.4 0.1 pad_add_fusion
  421.4 0.1 dynamic_slice.3
  421.5 0.1 compare_convert_fusion.1
  421.6 0.0 copy-done.3
  421.6 315.4 %all_gather.11 = bf16[3,1024,128]{2,1,0:T(8,128)(2,1)S(1)} all-gather(bf16[3,16,128]{2,1,0:T(8,128)(2,1)S(1)} %copy-done.3), channel_id=1, replica_groups=mesh['frame'=8,'row'=8,'col'=8] {'frame','row'}, dimensions={1}, use_global_device_ids=true | all-gather | bytes 798720 | tf_op jit(solution)/shard_map/all_gather | solution.py:52
  737.1 3.6 convolution_multiply_fusion
  740.7 0.0 copy-done.4
  740.7 3.5 fusion.19
  744.1 0.0 copy-done
  744.2 2.1 fusion.26
  (4 shorter events, 0.0 us)
Async XLA Ops:
  7.4 5.7 collective-permute-start
  11.3 6.2 collective-permute-start.1
  22.2 127.3 %all-to-all-start = ((bf16[8,4,10,64,128]{4,3,2,1,0:T(8,128)(2,1)}), bf16[8,4,10,64,128]{4,3,2,1,0:T(8,128)(2,1)}, u32[]{:S(2)}, u32[]{:S(2)}) async-start(bf16[8,4,10,64,128]{4,3,2,1,0:T(8,128)(2,1)} %stack.2), calls=%async_computation | async-start | bytes 10485760 | tf_op jit(solution)/shard_map/all_to_all | solution.py:46
  39.4 351.9 %all-gather.3.cloned.1.call-start = ((), (), s32[]{:S(2)}) async-start(), calls=%async_computation.1 | async-start | bytes 2396160 | tf_op jit(solution)/shard_map/all_gather | solution.py:51
  40.1 696.9 %all-gather.5.cloned.1.call-start = ((), (), s32[]{:S(2)}) async-start(), calls=%async_computation.2 | async-start | bytes 7077888 | tf_op jit(solution)/shard_map/all_gather | solution.py:64
  391.3 3.8 copy-start.1
  391.3 6.1 copy-start.2
  406.0 3.5 copy-start.5
  409.5 11.8 %copy-start.6 = (s32[32]{0:T(128)S(1)}, s32[32]{0:T(128)}, u32[]{:S(2)}) copy-start(s32[32]{0:T(128)} %param.11) | copy-start | bytes 388
  409.5 12.1 %copy-start.3 = (bf16[3,16,128]{2,1,0:T(8,128)(2,1)S(1)}, bf16[3,16,128]{2,1,0:T(8,128)(2,1)}, u32[]{:S(2)}) copy-start(bf16[3,16,128]{2,1,0:T(8,128)(2,1)} %param.8) | copy-start | bytes 36868
  413.1 327.6 %copy-start.4 = (f32[128]{0:T(128)S(1)}, f32[128]{0:T(128)}, u32[]{:S(2)}) copy-start(f32[128]{0:T(128)} %param.10) | copy-start | bytes 1540
  413.1 3.7 collective-permute-start.2
  415.3 5.0 collective-permute-start.3
  737.0 7.1 copy-start
Sparse Core Ops, SparseCore 0:
  42.2 349.0 all-gather.2
  421.5 249.7 all-gather.4
